TPU v7x, 32 devices: a whole 2x2x4 slice. The times are simulated.
32 devices in a mesh: group: 2 (over y), tm: 4 (over x, core), space: 4 (over z).
Axes of the slice: x: 2, y: 2, z: 4, core: 2. Of those that a mesh axis runs over, the one named last changes fastest.
Arguments:
- start_latent: float32 [32, 32, 256], P('group', 'space'), parts along dimension 0, may hold values from -6 to 6
- time_embed: float32 [8, 128], P('tm'), may hold values from -6 to 6
- drift_x: float32 [8], P('tm'), may hold values from -0.06 to -0.01
- drift_eps: float32 [8], P('tm'), may hold values from 0.02 to 0.1
- w_in: float32 [3, 3, 128, 16], replicated, may hold values from -0.5 to 0.5
- b_in: float32 [128], replicated, may hold values from -3 to 3
- w_mid: float32 [3, 3, 128, 128], replicated, may hold values from -0.1875 to 0.1875
- b_mid: float32 [128], replicated, may hold values from -3 to 3
- w_out: float32 [3, 3, 16, 128], replicated, may hold values from -0.1875 to 0.1875
- b_out: float32 [16], replicated, may hold values from -3 to 3
Outputs:
- trajectory: float32 [8, 32, 32, 256], P('tm', 'group', 'space'), parts along dimension 1
There are 2 independent parts, one for each index of `group`. A program takes and returns all parts, laid end to end along the dimension named above; an argument that names none is the same for every part. Nothing has to cross between parts.
All inputs are finite; a program needn't handle non-finite values.
Results may differ from a plain program's by a relative error of at most 0.0001.
Values sent between devices are 32-bit elements; how exact they have to be, the bound alone decides.
A program may use at most 64 MiB of HBM per device.

v0:
```python
import functools
import jax
import jax.numpy as jnp
from jax import lax
from jax.experimental import pallas as pl
from jax.experimental.pallas import tpu as pltpu
from jax.sharding import PartitionSpec as P

ITERS = 2
HALO = 3
BF = jnp.bfloat16
F32 = jnp.float32


def split(v):
    hi = v.astype(BF)
    lo = (v - hi.astype(F32)).astype(BF)
    return hi, lo


def shifted(v):
    cols = v.shape[1]
    lane = lax.broadcasted_iota(jnp.int32, v.shape, 1)
    left = jnp.where(lane == 0, 0.0, pltpu.roll(v, 1, 1))
    right = jnp.where(lane == cols - 1, 0.0, pltpu.roll(v, cols - 1, 1))
    return left, v, right


def dot(a, b):
    return jnp.dot(a, b, preferred_element_type=F32)


def silu(u):
    half = 0.5 * u
    return half + half * jnp.tanh(half)


def column(row, n):
    return jnp.transpose(jnp.broadcast_to(row, (n, row.shape[1])))


def wide(m, cols):
    return jnp.concatenate([m] * (cols // m.shape[1]), axis=1)


def denoise_kernel(shared, x_ref, te_ref, dx_ref, de_ref, win_ref, bin_ref, wmid_ref, bmid_ref, wout_ref, bout_ref,
                   out_ref, w0, w1, w2, bias, bias_out, s0h, s0l, s1h, s1l, acc):
    states, chans, rows, cols = out_ref.shape
    hid = wmid_ref.shape[2]
    fields = x_ref.shape[0]
    ext = rows + 2 * HALO
    space = lax.axis_index("space")
    height = rows * lax.axis_size("space")
    base = space * rows

    hi, lo = split(win_ref[...])
    w0[0:hid, :] = hi
    w0[hid:2 * hid, :] = lo
    for a in range(3):
        for b in range(3):
            hi, lo = split(wmid_ref[a, b])
            k = (a * 3 + b) * hid
            w1[0:hid, k:k + hid] = hi
            w1[hid:2 * hid, k:k + hid] = lo
    taps = 9 * chans
    for b in range(3):
        for a in range(3):
            hi, lo = split(wout_ref[a, b])
            m = (b * 3 + 2 - a) * chans
            w2[m:m + chans, 0:hid] = hi
            w2[m:m + chans, hid:2 * hid] = hi
            w2[taps + m:taps + m + chans, 0:hid] = lo
            w2[taps + m:taps + m + chans, hid:2 * hid] = lo
    for t in range(states):
        bias[t] = column(bin_ref[...] + te_ref[t:t + 1, :], 128)
    bias[states] = column(bmid_ref[...], 128)

    for t in range(fields):
        for r in range(ext):
            parts = shifted(x_ref[t, :, r, :])
            for b in range(3):
                hi, lo = split(parts[b])
                at = r * 3 * chans + b * chans
                s0h[t, at:at + chans, :] = hi
                s0l[t, at:at + chans, :] = lo
    acc[...] = jnp.zeros_like(acc)

    def first(r):
        k0 = 3 * chans
        at = pl.multiple_of(r * k0, 16)
        grow = base + r - (HALO - 1)
        keep = jnp.where((grow >= 0) & (grow < height), 1.0, 0.0).astype(F32)
        for t in range(states):
            if t < fields:
                f = dot(w0[...], s0h[t, pl.ds(at, 3 * k0), :])
                pre = f[:hid] + f[hid:] + dot(w0[0:hid, :], s0l[t, pl.ds(at, 3 * k0), :])
            h = silu(pre + wide(bias[t], cols)) * keep
            parts = shifted(h)
            for b in range(3):
                hi, lo = split(parts[b])
                to = pl.multiple_of(r * 3 * hid + b * hid, 128)
                s1h[t, pl.ds(to, hid), :] = hi
                s1l[t, pl.ds(to, hid), :] = lo

    def second(q):
        k1 = 3 * hid
        at = pl.multiple_of(q * k1, 128)
        grow = base + q - (HALO - 2)
        keep = jnp.where((grow >= 0) & (grow < height), 1.0, 0.0).astype(F32)
        for t in range(states):
            f = dot(w1[...], s1h[t, pl.ds(at, 3 * k1), :])
            pre = f[:hid] + f[hid:] + dot(w1[0:hid, :], s1l[t, pl.ds(at, 3 * k1), :])
            h = silu(pre + wide(bias[states], cols)) * keep
            hi, lo = split(h)
            g = dot(w2[...], jnp.concatenate([hi, lo], axis=0))
            g = g[:taps] + g[taps:]
            third = taps // 3
            left, _, _ = shifted(g[:third])
            _, _, right = shifted(g[2 * third:])
            to = pl.multiple_of(q * chans, 16)
            acc[t, pl.ds(to, third), :] += left + g[third:2 * third] + right

    def lap0(r, c):
        first(r)
        return c

    def lap(r, c):
        second(r - 3)
        first(r)
        return c

    lax.fori_loop(0, 3, lap0, 0)
    lax.fori_loop(3, rows + 4, lap, 0)
    second(rows + 1)

    for h in range(rows):
        total = None
        for t in range(states):
            noise = acc[t, (h + 2) * chans:(h + 3) * chans, :] + wide(bout_ref[...], cols)
            d = dx_ref[t] * x_ref[min(t, fields - 1), :, h + HALO, :] + de_ref[t] * noise
            total = d if total is None else total + d
            out_ref[t, :, h, :] = total


def denoise(x, te, dx, de, win, bin_, wmid, bmid, wout, bout, rows):
    fields, chans, ext, cols = x.shape
    states = te.shape[0]
    hid = wmid.shape[2]
    vm = pl.BlockSpec(memory_space=pltpu.VMEM)
    sm = pl.BlockSpec(memory_space=pltpu.SMEM)
    return pl.pallas_call(
        functools.partial(denoise_kernel, fields == 1),
        out_shape=jax.ShapeDtypeStruct((states, chans, rows, cols), F32),
        in_specs=[vm, vm, sm, sm, vm, vm, vm, vm, vm, vm],
        out_specs=vm,
        scratch_shapes=[
            pltpu.VMEM((2 * hid, 9 * chans), BF),
            pltpu.VMEM((2 * hid, 9 * hid), BF),
            pltpu.VMEM((18 * chans, 2 * hid), BF),
            pltpu.VMEM((states + 1, hid, 128), F32),
            pltpu.VMEM((chans, 128), F32),
            pltpu.VMEM((fields, ext * 3 * chans, cols), BF),
            pltpu.VMEM((fields, ext * 3 * chans, cols), BF),
            pltpu.VMEM((states, (rows + 4) * 3 * hid, cols), BF),
            pltpu.VMEM((states, (rows + 4) * 3 * hid, cols), BF),
            pltpu.VMEM((states, (rows + 4) * chans, cols), F32),
        ],
        compiler_params=pltpu.CompilerParams(vmem_limit_bytes=40 * 1024 * 1024),
        name="denoise",
    )(x, te, dx, de, win, bin_, wmid, bmid, wout, bout)


def halo_rows(v, dim):
    count = lax.axis_size("space")
    n = v.shape[dim]
    head = lax.slice_in_dim(v, 0, HALO, axis=dim)
    tail = lax.slice_in_dim(v, n - HALO, n, axis=dim)
    up = lax.ppermute(tail, "space", [(i, i + 1) for i in range(count - 1)])
    down = lax.ppermute(head, "space", [(i + 1, i) for i in range(count - 1)])
    return jnp.concatenate([up, v, down], axis=dim)


def earlier_sum(v):
    count = lax.axis_size("tm")
    total = jnp.zeros_like(v)
    for j in range(1, count):
        total = total + lax.ppermute(v, "tm", [(i, i + j) for i in range(count - j)])
    return total


def on_device(start_latent, time_embed, drift_x, drift_eps, w_in, b_in, w_mid, b_mid, w_out, b_out):
    chans, rows, cols = start_latent.shape
    hid = w_mid.shape[2]
    win = jnp.transpose(w_in, (2, 0, 1, 3)).reshape(hid, 9 * chans)
    bout = jnp.broadcast_to(b_out[:, None], (chans, 128))
    weights = (win, b_in[None], w_mid, b_mid[None], w_out, bout)
    start_ext = halo_rows(start_latent, 1)
    inputs = start_ext[None]
    for iteration in range(ITERS):
        running = denoise(inputs, time_embed, drift_x, drift_eps, *weights, rows)
        if iteration + 1 < ITERS:
            run_ext = halo_rows(running, 2)
            first = start_ext + earlier_sum(run_ext[-1])
            inputs = jnp.concatenate([first[None], first[None] + run_ext[:-1]], 0)
        else:
            return (start_latent + earlier_sum(running[-1]))[None] + running


def solution(mesh):
    in_specs = (
        P("group", "space", None),
        P("tm", None),
        P("tm"),
        P("tm"),
        P(),
        P(),
        P(),
        P(),
        P(),
        P(),
    )
    out_specs = P("tm", "group", "space", None)
    return jax.shard_map(
        on_device, mesh=mesh, in_specs=in_specs, out_specs=out_specs, check_vma=False
    )
```

profile of v0, /device:TPU:1, one launch (start us, length us, event | category | flops | bytes accessed | tf_op | source)
XLA Modules:
  0.0 92.2 jit_solution(2806634122547154446)
XLA Ops:
  0.0 1.1 %fusion.2 = (f32[16,3,256]{2,1,0:T(4,128)S(1)}, f32[16,3,256]{2,1,0:T(4,128)S(1)}) fusion(f32[16,8,256]{2,1,0:T(8,128)} %param.10), kind=kLoop, calls=%fused_computation.11 | loop fusion | bytes 196608 | tf_op jit(solution)/shard_map/slice | solution.py:177
  1.1 4.0 %collective-permute-start = (f32[16,3,256]{2,1,0:T(4,128)S(1)}, f32[16,3,256]{2,1,0:T(4,128)S(1)}, u32[]{:S(2)}, u32[]{:S(2)}) collective-permute-start(f32[16,3,256]{2,1,0:T(4,128)S(1)} %get-tuple-element.9), channel_id=1, source_target_pairs={{0,1},{1,2},{2,3},{4,5},{5,6},{6,7},{8,9},{9,10},{10,11},{12,13},{... | collective-permute-start | bytes 147464 | tf_op jit(solution)/shard_map/ppermute | solution.py:178
  5.1 1.3 %collective-permute-start.1 = (f32[16,3,256]{2,1,0:T(4,128)S(1)}, f32[16,3,256]{2,1,0:T(4,128)S(1)}, u32[]{:S(2)}, u32[]{:S(2)}) collective-permute-start(f32[16,3,256]{2,1,0:T(4,128)S(1)} %get-tuple-element.10), channel_id=1, source_target_pairs={{1,0},{2,1},{3,2},{5,4},{6,5},{7,6},{9,8},{10,9},{11,10},{13,12},{... | collective-permute-start | bytes 147464 | tf_op jit(solution)/shard_map/ppermute | solution.py:179
  6.5 3.6 %collective-permute-done.1 = f32[16,3,256]{2,1,0:T(4,128)S(1)} collective-permute-done((f32[16,3,256]{2,1,0:T(4,128)S(1)}, f32[16,3,256]{2,1,0:T(4,128)S(1)}, u32[]{:S(2)}, u32[]{:S(2)}) %collective-permute-start.1) | collective-permute-done | bytes 49184 | tf_op jit(solution)/shard_map/ppermute | solution.py:179
  10.1 1.0 %fusion.x_ref = f32[1,16,14,256]{3,2,1,0:T(8,128)S(1)} fusion(f32[16,3,256]{2,1,0:T(4,128)S(1)} %collective-permute-done.1, f32[16,8,256]{2,1,0:T(8,128)} %param.10, f32[16,3,256]{2,1,0:T(4,128)S(1)} %collective-permute-done), kind=kLoop, calls=%fused_computation.6 | loop fusion | flops 114688 | bytes 458752 | tf_op jit(solution)/shard_map/broadcast_in_dim | solution.py:198
  11.1 0.6 copy-done.9
  11.8 0.6 copy-done.2
  12.4 21.8 %denoise.2 = f32[2,16,8,256]{3,2,1,0:T(8,128)S(1)} custom-call(f32[1,16,14,256]{3,2,1,0:T(8,128)S(1)} %fusion.x_ref, f32[2,128]{1,0:T(2,128)S(1)} %copy-done.2, f32[2]{0:T(128)S(1)} %copy-done.3, f32[2]{0:T(128)S(1)} %copy-done.4, f32[128,144]{1,0:T(8,128)S(1)} %copy.12.win_ref, f32[1,128]{1,0:T(1,128)S(1)} %bitcast.14, f32[3,3,128,128]{3,2,1,0:T(8,128)S(1)} %copy-done, ...), custom_call_target="tpu_custom_call" | custom-call | tf_op jit(solution)/shard_map/denoise/pallas_call | solution.py:151
  34.3 3.2 %collective-permute-start.2 = (f32[2,16,3,256]{3,2,1,0:T(4,128)S(1)}, f32[2,16,3,256]{3,2,1,0:T(4,128)S(1)}, u32[]{:S(2)}, u32[]{:S(2)}) collective-permute-start(f32[2,16,3,256]{3,2,1,0:T(4,128)S(1)} %get-tuple-element.7), channel_id=1, source_target_pairs={{0,1},{1,2},{2,3},{4,5},{5,6},{6,7},{8,9},{9,10},{10,11},{12,13},{... | collective-permute-start | bytes 294920 | tf_op jit(solution)/shard_map/ppermute | solution.py:178
  37.5 1.3 %collective-permute-start.3 = (f32[2,16,3,256]{3,2,1,0:T(4,128)S(1)}, f32[2,16,3,256]{3,2,1,0:T(4,128)S(1)}, u32[]{:S(2)}, u32[]{:S(2)}) collective-permute-start(f32[2,16,3,256]{3,2,1,0:T(4,128)S(1)} %get-tuple-element.8), channel_id=1, source_target_pairs={{1,0},{2,1},{3,2},{5,4},{6,5},{7,6},{9,8},{10,9},{11,10},{13,12},{... | collective-permute-start | bytes 294920 | tf_op jit(solution)/shard_map/ppermute | solution.py:179
  38.8 0.6 collective-permute-done.2
  39.5 3.8 %collective-permute-done.3 = f32[2,16,3,256]{3,2,1,0:T(4,128)S(1)} collective-permute-done((f32[2,16,3,256]{3,2,1,0:T(4,128)S(1)}, f32[2,16,3,256]{3,2,1,0:T(4,128)S(1)}, u32[]{:S(2)}, u32[]{:S(2)}) %collective-permute-start.3) | collective-permute-done | bytes 98336 | tf_op jit(solution)/shard_map/ppermute | solution.py:179
  43.4 0.8 collective-permute-start.6
  44.2 3.7 %collective-permute-start.5 = (f32[16,14,256]{2,1,0:T(8,128)S(1)}, f32[16,14,256]{2,1,0:T(8,128)S(1)}, u32[]{:S(2)}, u32[]{:S(2)}) collective-permute-start(f32[16,14,256]{2,1,0:T(8,128)S(1)} %slice_bitcast_fusion), channel_id=1, source_target_pairs={{0,8},{4,12},{1,9},{5,13},{2,10},{6,14},{3,11},{7,15},{16,24},{20,... | collective-permute-start | bytes 688136 | tf_op jit(solution)/shard_map/ppermute | solution.py:187
  48.0 4.1 %collective-permute-start.4 = (f32[16,14,256]{2,1,0:T(8,128)S(1)}, f32[16,14,256]{2,1,0:T(8,128)S(1)}, u32[]{:S(2)}, u32[]{:S(2)}) collective-permute-start(f32[16,14,256]{2,1,0:T(8,128)S(1)} %slice_bitcast_fusion), channel_id=1, source_target_pairs={{0,4},{4,8},{8,12},{1,5},{5,9},{9,13},{2,6},{6,10},{10,14},{3,7},{... | collective-permute-start | bytes 688136 | tf_op jit(solution)/shard_map/ppermute | solution.py:187
  52.1 1.4 %collective-permute-done.5 = f32[16,14,256]{2,1,0:T(8,128)S(1)} collective-permute-done((f32[16,14,256]{2,1,0:T(8,128)S(1)}, f32[16,14,256]{2,1,0:T(8,128)S(1)}, u32[]{:S(2)}, u32[]{:S(2)}) %collective-permute-start.5) | collective-permute-done | bytes 229408 | tf_op jit(solution)/shard_map/ppermute | solution.py:187
  53.5 5.6 %collective-permute-done.4 = f32[16,14,256]{2,1,0:T(8,128)S(1)} collective-permute-done((f32[16,14,256]{2,1,0:T(8,128)S(1)}, f32[16,14,256]{2,1,0:T(8,128)S(1)}, u32[]{:S(2)}, u32[]{:S(2)}) %collective-permute-start.4) | collective-permute-done | bytes 229408 | tf_op jit(solution)/shard_map/ppermute | solution.py:187
  59.1 0.1 slice_add_fusion
  59.3 22.6 %denoise.3 = f32[2,16,8,256]{3,2,1,0:T(8,128)S(1)} custom-call(f32[2,16,14,256]{3,2,1,0:T(8,128)S(1)} %pad_maximum_fusion.1.x_ref, f32[2,128]{1,0:T(2,128)S(1)} %copy-done.2, f32[2]{0:T(128)S(1)} %copy-done.3, f32[2]{0:T(128)S(1)} %copy-done.4, f32[128,144]{1,0:T(8,128)S(1)} %copy.12.win_ref, f32[1,128]{1,0:T(1,128)S(1)} %bitcast.15, ...), custom_call_target="tpu_custom_call" | custom-call | tf_op jit(solution)/shard_map/denoise/pallas_call | solution.py:151
  81.9 0.7 collective-permute-start.9
  82.6 1.3 %collective-permute-start.8 = (f32[16,8,256]{2,1,0:T(8,128)S(1)}, f32[16,8,256]{2,1,0:T(8,128)S(1)}, u32[]{:S(2)}, u32[]{:S(2)}) collective-permute-start(f32[16,8,256]{2,1,0:T(8,128)S(1)} %slice_bitcast_fusion.1), channel_id=1, source_target_pairs={{0,8},{4,12},{1,9},{5,13},{2,10},{6,14},{3,11},{7,15},{16,24},{20,... | collective-permute-start | bytes 393224 | tf_op jit(solution)/shard_map/ppermute | solution.py:187
  83.9 5.0 %collective-permute-start.7 = (f32[16,8,256]{2,1,0:T(8,128)S(1)}, f32[16,8,256]{2,1,0:T(8,128)S(1)}, u32[]{:S(2)}, u32[]{:S(2)}) collective-permute-start(f32[16,8,256]{2,1,0:T(8,128)S(1)} %slice_bitcast_fusion.1), channel_id=1, source_target_pairs={{0,4},{4,8},{8,12},{1,5},{5,9},{9,13},{2,6},{6,10},{10,14},{3,7},{... | collective-permute-start | bytes 393224 | tf_op jit(solution)/shard_map/ppermute | solution.py:187
  88.9 2.5 %collective-permute-done.7 = f32[16,8,256]{2,1,0:T(8,128)S(1)} collective-permute-done((f32[16,8,256]{2,1,0:T(8,128)S(1)}, f32[16,8,256]{2,1,0:T(8,128)S(1)}, u32[]{:S(2)}, u32[]{:S(2)}) %collective-permute-start.7) | collective-permute-done | bytes 131104 | tf_op jit(solution)/shard_map/ppermute | solution.py:187
  91.5 0.7 broadcast_add_fusion
  (30 shorter events, 0.5 us)
Async XLA Ops:
  0.0 6.4 %copy-start.8 = (f32[3,3,128,16]{2,3,1,0:T(8,128)S(1)}, f32[3,3,128,16]{2,3,1,0:T(8,128)}, u32[]{:S(2)}) copy-start(f32[3,3,128,16]{2,3,1,0:T(8,128)} %param.14) | copy-start | bytes 221188
  0.0 11.8 %copy-start = (f32[3,3,128,128]{3,2,1,0:T(8,128)S(1)}, f32[3,3,128,128]{3,2,1,0:T(8,128)}, u32[]{:S(2)}) copy-start(f32[3,3,128,128]{3,2,1,0:T(8,128)} %wmid_ref.3) | copy-start | bytes 1769476
  1.1 5.5 %collective-permute-start = (f32[16,3,256]{2,1,0:T(4,128)S(1)}, f32[16,3,256]{2,1,0:T(4,128)S(1)}, u32[]{:S(2)}, u32[]{:S(2)}) collective-permute-start(f32[16,3,256]{2,1,0:T(4,128)S(1)} %get-tuple-element.9), channel_id=1, source_target_pairs={{0,1},{1,2},{2,3},{4,5},{5,6},{6,7},{8,9},{9,10},{10,11},{12,13},{... | collective-permute-start | bytes 147464 | tf_op jit(solution)/shard_map/ppermute | solution.py:178
  5.1 5.0 %collective-permute-start.1 = (f32[16,3,256]{2,1,0:T(4,128)S(1)}, f32[16,3,256]{2,1,0:T(4,128)S(1)}, u32[]{:S(2)}, u32[]{:S(2)}) collective-permute-start(f32[16,3,256]{2,1,0:T(4,128)S(1)} %get-tuple-element.10), channel_id=1, source_target_pairs={{1,0},{2,1},{3,2},{5,4},{6,5},{7,6},{9,8},{10,9},{11,10},{13,12},{... | collective-permute-start | bytes 147464 | tf_op jit(solution)/shard_map/ppermute | solution.py:179
  6.5 5.3 %copy-start.1 = (f32[3,3,16,128]{3,2,1,0:T(8,128)S(1)}, f32[3,3,16,128]{3,2,1,0:T(8,128)}, u32[]{:S(2)}) copy-start(f32[3,3,16,128]{3,2,1,0:T(8,128)} %wout_ref.3) | copy-start | bytes 221188
  11.1 0.7 copy-start.9
  11.7 0.7 copy-start.2
  11.7 0.7 copy-start.3
  11.7 0.7 copy-start.4
  11.7 0.7 copy-start.5
  11.7 0.7 copy-start.6
  34.3 5.1 %collective-permute-start.2 = (f32[2,16,3,256]{3,2,1,0:T(4,128)S(1)}, f32[2,16,3,256]{3,2,1,0:T(4,128)S(1)}, u32[]{:S(2)}, u32[]{:S(2)}) collective-permute-start(f32[2,16,3,256]{3,2,1,0:T(4,128)S(1)} %get-tuple-element.7), channel_id=1, source_target_pairs={{0,1},{1,2},{2,3},{4,5},{5,6},{6,7},{8,9},{9,10},{10,11},{12,13},{... | collective-permute-start | bytes 294920 | tf_op jit(solution)/shard_map/ppermute | solution.py:178
  37.5 5.7 %collective-permute-start.3 = (f32[2,16,3,256]{3,2,1,0:T(4,128)S(1)}, f32[2,16,3,256]{3,2,1,0:T(4,128)S(1)}, u32[]{:S(2)}, u32[]{:S(2)}) collective-permute-start(f32[2,16,3,256]{3,2,1,0:T(4,128)S(1)} %get-tuple-element.8), channel_id=1, source_target_pairs={{1,0},{2,1},{3,2},{5,4},{6,5},{7,6},{9,8},{10,9},{11,10},{13,12},{... | collective-permute-start | bytes 294920 | tf_op jit(solution)/shard_map/ppermute | solution.py:179
  43.3 15.7 %copy-start.7 = (f32[16,8,256]{2,1,0:T(8,128)S(1)}, f32[16,8,256]{2,1,0:T(8,128)}, u32[]{:S(2)}) copy-start(f32[16,8,256]{2,1,0:T(8,128)} %param.10) | copy-start | bytes 393220
  43.4 8.7 %collective-permute-start.6 = (f32[16,14,256]{2,1,0:T(8,128)S(1)}, f32[16,14,256]{2,1,0:T(8,128)S(1)}, u32[]{:S(2)}, u32[]{:S(2)}) collective-permute-start(f32[16,14,256]{2,1,0:T(8,128)S(1)} %slice_bitcast_fusion), channel_id=1, source_target_pairs={{0,12},{1,13},{2,14},{3,15},{16,28},{17,29},{18,30},{19,31}} | collective-permute-start | bytes 688136 | tf_op jit(solution)/shard_map/ppermute | solution.py:187
  44.2 9.3 %collective-permute-start.5 = (f32[16,14,256]{2,1,0:T(8,128)S(1)}, f32[16,14,256]{2,1,0:T(8,128)S(1)}, u32[]{:S(2)}, u32[]{:S(2)}) collective-permute-start(f32[16,14,256]{2,1,0:T(8,128)S(1)} %slice_bitcast_fusion), channel_id=1, source_target_pairs={{0,8},{4,12},{1,9},{5,13},{2,10},{6,14},{3,11},{7,15},{16,24},{20,... | collective-permute-start | bytes 688136 | tf_op jit(solution)/shard_map/ppermute | solution.py:187
  48.0 11.1 %collective-permute-start.4 = (f32[16,14,256]{2,1,0:T(8,128)S(1)}, f32[16,14,256]{2,1,0:T(8,128)S(1)}, u32[]{:S(2)}, u32[]{:S(2)}) collective-permute-start(f32[16,14,256]{2,1,0:T(8,128)S(1)} %slice_bitcast_fusion), channel_id=1, source_target_pairs={{0,4},{4,8},{8,12},{1,5},{5,9},{9,13},{2,6},{6,10},{10,14},{3,7},{... | collective-permute-start | bytes 688136 | tf_op jit(solution)/shard_map/ppermute | solution.py:187
  81.9 7.0 %collective-permute-start.9 = (f32[16,8,256]{2,1,0:T(8,128)S(1)}, f32[16,8,256]{2,1,0:T(8,128)S(1)}, u32[]{:S(2)}, u32[]{:S(2)}) collective-permute-start(f32[16,8,256]{2,1,0:T(8,128)S(1)} %slice_bitcast_fusion.1), channel_id=1, source_target_pairs={{0,12},{1,13},{2,14},{3,15},{16,28},{17,29},{18,30},{19,31}} | collective-permute-start | bytes 393224 | tf_op jit(solution)/shard_map/ppermute | solution.py:187
  82.6 6.3 %collective-permute-start.8 = (f32[16,8,256]{2,1,0:T(8,128)S(1)}, f32[16,8,256]{2,1,0:T(8,128)S(1)}, u32[]{:S(2)}, u32[]{:S(2)}) collective-permute-start(f32[16,8,256]{2,1,0:T(8,128)S(1)} %slice_bitcast_fusion.1), channel_id=1, source_target_pairs={{0,8},{4,12},{1,9},{5,13},{2,10},{6,14},{3,11},{7,15},{16,24},{20,... | collective-permute-start | bytes 393224 | tf_op jit(solution)/shard_map/ppermute | solution.py:187
  83.9 7.6 %collective-permute-start.7 = (f32[16,8,256]{2,1,0:T(8,128)S(1)}, f32[16,8,256]{2,1,0:T(8,128)S(1)}, u32[]{:S(2)}, u32[]{:S(2)}) collective-permute-start(f32[16,8,256]{2,1,0:T(8,128)S(1)} %slice_bitcast_fusion.1), channel_id=1, source_target_pairs={{0,4},{4,8},{8,12},{1,5},{5,9},{9,13},{2,6},{6,10},{10,14},{3,7},{... | collective-permute-start | bytes 393224 | tf_op jit(solution)/shard_map/ppermute | solution.py:187
where the time goes:
time: 92.6 us; the launch traced here: 92.2 us
  Pallas kernels  44.4 us (48%)
  starting transfers between devices  25.4 us (27%)
  waiting for transfers between devices  17.6 us (19%)
  local copies, waits for them, and re-layouts  2.59 us (3%)
  other arithmetic  1.99 us (2%)
    pallas_call x2, Pallas kernels, denoise(): pl.pallas_call(functools.partial(denoise_kernel, fields == 1), out_shape=...  44.4 us
    ppermute x6, starting transfers between devices, earlier_sum(): lax.ppermute(v, 'tm', [(i, i + j) for i in range(count - j)])  15.6 us
    ppermute x6, waiting for transfers between devices, earlier_sum(): lax.ppermute(v, 'tm', [(i, i + j) for i in range(count - j)])  9.57 us
    ppermute x2, waiting for transfers between devices, halo_rows(): down = lax.ppermute(head, 'space', [(i + 1, i) for i in range(count - 1)])  7.36 us
    ppermute x2, starting transfers between devices, halo_rows(): up = lax.ppermute(tail, 'space', [(i, i + 1) for i in range(count - 1)])  7.23 us
    ppermute x2, starting transfers between devices, halo_rows(): down = lax.ppermute(head, 'space', [(i + 1, i) for i in range(count - 1)])  2.58 us
  transfers between devices with their start and end apart: 10, of which 6 were waited for; matrix products, arithmetic and copies ran while one was open for 0% of the time, Pallas kernels for 0%

commit v1 on v0

v1 whole, which is shorter than its diff:
```python
import functools
import jax
import jax.numpy as jnp
from jax import lax
from jax.experimental import pallas as pl
from jax.experimental.pallas import tpu as pltpu
from jax.sharding import PartitionSpec as P

HALO = 3
BF = jnp.bfloat16
F32 = jnp.float32


def split(v):
    hi = v.astype(BF)
    lo = (v - hi.astype(F32)).astype(BF)
    return hi, lo


def shifted(v):
    cols = v.shape[1]
    lane = lax.broadcasted_iota(jnp.int32, v.shape, 1)
    left = jnp.where(lane == 0, 0.0, pltpu.roll(v, 1, 1))
    right = jnp.where(lane == cols - 1, 0.0, pltpu.roll(v, cols - 1, 1))
    return left, v, right


def dot(a, b):
    return jnp.dot(a, b, preferred_element_type=F32)


def silu(u):
    half = 0.5 * u
    return half + half * jnp.tanh(half)


def column(row, n):
    return jnp.transpose(jnp.broadcast_to(row, (n, row.shape[1])))


def wide(m, cols):
    return jnp.concatenate([m] * (cols // m.shape[1]), axis=1)


MESH = pl.DeviceIdType.MESH


def picard_kernel(start_ref, te_ref, dx_ref, de_ref, win_ref, bin_ref, wmid_ref, bmid_ref, wout_ref, bout_ref,
                  out_ref, w0, w1, w2, bias, s0h, s0l, s1h, s1l, acc, x0, xin, run, car, snd, run2, car2, snd2,
                  hs_send, hs_recv, hr_send, hr_recv, c_send, c_recv, f_send, f_recv):
    states, chans, rows, cols = out_ref.shape
    hid = wmid_ref.shape[2]
    ext = rows + 2 * HALO
    space, spaces = lax.axis_index("space"), lax.axis_size("space")
    tm, tms = lax.axis_index("tm"), lax.axis_size("tm")
    height = rows * spaces
    base = space * rows
    has_up, has_down = space < spaces - 1, space > 0
    has_next, has_prev = tm < tms - 1, tm > 0
    up, down, nxt, prv = {"space": space + 1}, {"space": space - 1}, {"tm": tm + 1}, {"tm": tm - 1}

    barrier = pltpu.get_barrier_semaphore()
    sides = ((has_up, up), (has_down, down), (has_next, nxt), (has_prev, prv))
    for there, who in sides:
        @pl.when(there)
        def _(who=who):
            pl.semaphore_signal(barrier, inc=1, device_id=who, device_id_type=MESH)

    for r in range(rows):
        x0[r + HALO] = start_ref[:, r, :]

    peers = sum(jnp.where(there, 1, 0) for there, _ in sides)
    pl.semaphore_wait(barrier, peers)

    def remote(src, dst, send, recv, who):
        return pltpu.make_async_remote_copy(src_ref=src, dst_ref=dst, send_sem=send, recv_sem=recv,
                                            device_id=who, device_id_type=MESH)

    def halo_pair(make, lead):
        top, tail = lead + (pl.ds(0, HALO),), lead + (pl.ds(rows, HALO),)
        first, bottom = lead + (pl.ds(HALO, HALO),), lead + (pl.ds(rows + HALO, HALO),)
        buf, send, recv = make
        go_up = remote(buf.at[tail], buf.at[top], send.at[0], recv.at[0], up)
        go_down = remote(buf.at[first], buf.at[bottom], send.at[1], recv.at[1], down)
        return go_up, go_down, top, bottom

    def halo_start(make, lead):
        go_up, go_down, top, bottom = halo_pair(make, lead)
        buf = make[0]

        @pl.when(has_up)
        def _():
            go_up.start()

        @pl.when(has_down)
        def _():
            go_down.start()

        @pl.when(jnp.logical_not(has_down))
        def _():
            buf[top] = jnp.zeros(buf.at[top].shape, F32)

        @pl.when(jnp.logical_not(has_up))
        def _():
            buf[bottom] = jnp.zeros(buf.at[bottom].shape, F32)

    def halo_wait(make, lead):
        go_up, go_down, top, bottom = halo_pair(make, lead)

        @pl.when(has_up)
        def _():
            go_up.wait_send()
            go_down.wait_recv()

        @pl.when(has_down)
        def _():
            go_down.wait_send()
            go_up.wait_recv()

    start_halo = ((x0, hs_send, hs_recv), ())
    run_halo = ((run, hr_send, hr_recv), (slice(None),))
    halo_start(*start_halo)

    hi, lo = split(win_ref[...])
    w0[0:hid, :] = hi
    w0[hid:2 * hid, :] = lo
    for a in range(3):
        for b in range(3):
            hi, lo = split(wmid_ref[a, b])
            k = (a * 3 + b) * hid
            w1[0:hid, k:k + hid] = hi
            w1[hid:2 * hid, k:k + hid] = lo
    taps = 9 * chans
    for b in range(3):
        for a in range(3):
            hi, lo = split(wout_ref[a, b])
            m = (b * 3 + 2 - a) * chans
            w2[m:m + chans, 0:hid] = hi
            w2[m:m + chans, hid:2 * hid] = hi
            w2[taps + m:taps + m + chans, 0:hid] = lo
            w2[taps + m:taps + m + chans, hid:2 * hid] = lo
    for t in range(states):
        bias[t] = column(bin_ref[...] + te_ref[t:t + 1, :], 128)
    bias[states] = column(bmid_ref[...], 128)

    def place(t, r, v):
        parts = shifted(v)
        for b in range(3):
            hi, lo = split(parts[b])
            at = r * 3 * chans + b * chans
            s0h[t, at:at + chans, :] = hi
            s0l[t, at:at + chans, :] = lo

    inner = list(range(HALO, HALO + rows))
    outer = list(range(HALO)) + list(range(HALO + rows, ext))

    def network(fields):
        acc[...] = jnp.zeros_like(acc)

        def first(r):
            k0 = 3 * chans
            at = pl.multiple_of(r * k0, 16)
            grow = base + r - (HALO - 1)
            keep = jnp.where((grow >= 0) & (grow < height), 1.0, 0.0).astype(F32)
            for t in range(states):
                if t < fields:
                    f = dot(w0[...], s0h[t, pl.ds(at, 3 * k0), :])
                    pre = f[:hid] + f[hid:] + dot(w0[0:hid, :], s0l[t, pl.ds(at, 3 * k0), :])
                h = silu(pre + wide(bias[t], cols)) * keep
                parts = shifted(h)
                for b in range(3):
                    hi, lo = split(parts[b])
                    to = pl.multiple_of(r * 3 * hid + b * hid, 128)
                    s1h[t, pl.ds(to, hid), :] = hi
                    s1l[t, pl.ds(to, hid), :] = lo

        def second(q):
            k1 = 3 * hid
            at = pl.multiple_of(q * k1, 128)
            grow = base + q - (HALO - 2)
            keep = jnp.where((grow >= 0) & (grow < height), 1.0, 0.0).astype(F32)
            for t in range(states):
                f = dot(w1[...], s1h[t, pl.ds(at, 3 * k1), :])
                pre = f[:hid] + f[hid:] + dot(w1[0:hid, :], s1l[t, pl.ds(at, 3 * k1), :])
                h = silu(pre + wide(bias[states], cols)) * keep
                hi, lo = split(h)
                g = dot(w2[...], jnp.concatenate([hi, lo], axis=0))
                g = g[:taps] + g[taps:]
                third = taps // 3
                left, _, _ = shifted(g[:third])
                _, _, right = shifted(g[2 * third:])
                to = pl.multiple_of(q * chans, 16)
                acc[t, pl.ds(to, third), :] += left + g[third:2 * third] + right

        def lap0(r, c):
            first(r)
            return c

        def lap(r, c):
            second(r - 3)
            first(r)
            return c

        lax.fori_loop(0, 3, lap0, 0)
        lax.fori_loop(3, rows + 4, lap, 0)
        second(rows + 1)

    def drifts(put, source):
        bo = wide(bout_ref[...], cols)
        for h in range(rows):
            total = None
            for t in range(states):
                noise = acc[t, (h + 2) * chans:(h + 3) * chans, :] + bo
                d = dx_ref[t] * source(t, h + HALO) + de_ref[t] * noise
                total = d if total is None else total + d
                put(t, h, total)

    def chain(car_at, snd_at, mine, send, recv):
        copy = remote(snd_at, car_at, send, recv, nxt)

        @pl.when(has_prev)
        def _():
            copy.wait_recv()

            @pl.when(has_next)
            def _():
                snd_at[...] = car_at[...] + mine[...]

        @pl.when(jnp.logical_not(has_prev))
        def _():
            car_at[...] = jnp.zeros(car_at.shape, F32)
            snd_at[...] = mine[...]

        @pl.when(has_next)
        def _():
            copy.start()
        return copy

    for r in inner:
        place(0, r, x0[r])
    halo_wait(*start_halo)
    for r in outer:
        place(0, r, x0[r])
    network(1)

    def put1(t, h, v):
        run[t, h + HALO] = v

    drifts(put1, lambda t, r: x0[r])

    pieces = [pl.ds(HALO, rows), pl.ds(0, HALO), pl.ds(HALO + rows, HALO)]
    last = states - 1
    copies = []

    def link(n):
        at = pieces[n]
        copies.append(chain(car.at[at], snd.at[at], run.at[last, at], c_send.at[n], c_recv.at[n]))

    def build(rs):
        for r in rs:
            first_in = x0[r] + car[r]
            for t in range(states):
                v = first_in if t == 0 else first_in + run[t - 1, r]
                xin[t, r] = v
                place(t, r, v)

    halo_start(*run_halo)
    link(0)
    halo_wait(*run_halo)
    link(1)
    link(2)
    build(inner)
    build(outer)
    network(states)

    def put2(t, h, v):
        run2[t, h] = v

    drifts(put2, lambda t, r: xin[t, r])
    parts = f_send.shape[0]
    size = rows // parts
    for n in range(parts):
        at = pl.ds(n * size, size)
        copies.append(chain(car2.at[at], snd2.at[at], run2.at[last, at], f_send.at[n], f_recv.at[n]))
        for h in range(n * size, (n + 1) * size):
            first_in = x0[h + HALO] + car2[h]
            for t in range(states):
                out_ref[t, :, h, :] = first_in + run2[t, h]

    @pl.when(has_next)
    def _():
        for copy in copies:
            copy.wait_send()


def picard(start, te, dx, de, win, bin_, wmid, bmid, wout, bout):
    chans, rows, cols = start.shape
    ext = rows + 2 * HALO
    states = te.shape[0]
    hid = wmid.shape[2]
    parts = 2 if rows % 2 == 0 else 1
    vm = pl.BlockSpec(memory_space=pltpu.VMEM)
    sm = pl.BlockSpec(memory_space=pltpu.SMEM)
    dma = pltpu.SemaphoreType.DMA
    return pl.pallas_call(
        picard_kernel,
        out_shape=jax.ShapeDtypeStruct((states, chans, rows, cols), F32),
        in_specs=[vm, vm, sm, sm, vm, vm, vm, vm, vm, vm],
        out_specs=vm,
        scratch_shapes=[
            pltpu.VMEM((2 * hid, 9 * chans), BF),
            pltpu.VMEM((2 * hid, 9 * hid), BF),
            pltpu.VMEM((18 * chans, 2 * hid), BF),
            pltpu.VMEM((states + 1, hid, 128), F32),
            pltpu.VMEM((states, ext * 3 * chans, cols), BF),
            pltpu.VMEM((states, ext * 3 * chans, cols), BF),
            pltpu.VMEM((states, (rows + 4) * 3 * hid, cols), BF),
            pltpu.VMEM((states, (rows + 4) * 3 * hid, cols), BF),
            pltpu.VMEM((states, (rows + 4) * chans, cols), F32),
            pltpu.VMEM((ext, chans, cols), F32),
            pltpu.VMEM((states, ext, chans, cols), F32),
            pltpu.VMEM((states, ext, chans, cols), F32),
            pltpu.VMEM((ext, chans, cols), F32),
            pltpu.VMEM((ext, chans, cols), F32),
            pltpu.VMEM((states, rows, chans, cols), F32),
            pltpu.VMEM((rows, chans, cols), F32),
            pltpu.VMEM((rows, chans, cols), F32),
            dma((2,)), dma((2,)), dma((2,)), dma((2,)), dma((3,)), dma((3,)), dma((parts,)), dma((parts,)),
        ],
        compiler_params=pltpu.CompilerParams(
            vmem_limit_bytes=48 * 1024 * 1024, collective_id=0, has_side_effects=True),
        name="picard",
    )(start, te, dx, de, win, bin_, wmid, bmid, wout, bout)


def on_device(start_latent, time_embed, drift_x, drift_eps, w_in, b_in, w_mid, b_mid, w_out, b_out):
    chans = start_latent.shape[0]
    hid = w_mid.shape[2]
    win = jnp.transpose(w_in, (2, 0, 1, 3)).reshape(hid, 9 * chans)
    bout = jnp.broadcast_to(b_out[:, None], (chans, 128))
    return picard(start_latent, time_embed, drift_x, drift_eps, win, b_in[None], w_mid, b_mid[None], w_out, bout)


def solution(mesh):
    in_specs = (
        P("group", "space", None),
        P("tm", None),
        P("tm"),
        P("tm"),
        P(),
        P(),
        P(),
        P(),
        P(),
        P(),
    )
    out_specs = P("tm", "group", "space", None)
    return jax.shard_map(
        on_device, mesh=mesh, in_specs=in_specs, out_specs=out_specs, check_vma=False
    )
```

time: 92.6 us -> 60.3 us (0.65)
  the two profiles are of different devices: /device:TPU:1 before, /device:TPU:3 now
where the time goes in v1:
time: 60.3 us; the launch traced here: 60.1 us
  Pallas kernels  56.4 us (94%)
  local copies, waits for them, and re-layouts  3.61 us (6%)
    pallas_call x1, Pallas kernels, picard(): pl.pallas_call(picard_kernel, out_shape=jax.ShapeDtypeStruct((states, cha...  56.4 us
    unnamed x17, local copies, waits for them, and re-layouts  1.8 us

profile of v1, /device:TPU:3, one launch (start us, length us, event | category | flops | bytes accessed | tf_op | source)
XLA Modules:
  0.0 60.1 jit_solution(17191821965763580662)
XLA Ops:
  0.0 0.0 copy-start.1
  0.0 0.8 %broadcast_in_dim.14.bout_ref = f32[16,128]{1,0:T(8,128)S(1)} broadcast(f32[16]{0:T(128)} %param.19), dimensions={0} | broadcast | bytes 8256 | tf_op jit(solution)/shard_map/broadcast_in_dim | solution.py:340
  0.8 0.0 copy-start.2
  0.8 0.0 copy-start.3
  0.8 0.0 copy-start.4
  0.8 0.0 copy-start.5
  0.8 0.0 copy-start.6
  0.8 0.0 copy-start.7
  0.8 1.1 %copy.12.win_ref = f32[128,144]{1,0:T(8,128)S(1)} copy(f32[128,144]{0,1:T(8,128)} %bitcast.7) | data formatting | bytes 147456 | tf_op jit(solution)/shard_map/reshape | solution.py:339
  1.9 0.0 copy-done.1
  1.9 0.0 copy-done.2
  1.9 0.0 copy-done.3
  1.9 0.0 copy-done.4
  1.9 0.0 copy-done.5
  1.9 0.0 copy-done.6
  1.9 0.0 copy-done.7
  1.9 0.0 copy-start
  1.9 1.1 %copy-done = f32[3,3,128,128]{3,2,1,0:T(8,128)S(1)} copy-done((f32[3,3,128,128]{3,2,1,0:T(8,128)S(1)}, f32[3,3,128,128]{3,2,1,0:T(8,128)}, u32[]{:S(2)}) %copy-start) | copy-done | bytes 589848
  3.0 56.4 %picard.1 = f32[2,16,8,256]{3,2,1,0:T(8,128)S(1)} custom-call(f32[16,8,256]{2,1,0:T(8,128)S(1)} %copy-done.1, f32[2,128]{1,0:T(2,128)S(1)} %copy-done.3, f32[2]{0:T(128)S(1)} %copy-done.4, f32[2]{0:T(128)S(1)} %copy-done.5, f32[128,144]{1,0:T(8,128)S(1)} %copy.12.win_ref, f32[1,128]{1,0:T(1,128)S(1)} %bitcast.5, f32[3,3,128,128]{3,2,1,0:T(8,128)S(1)} %copy-done, ...), custom_call_target="tpu_custom_call" | custom-call | tf_op jit(solution)/shard_map/picard/pallas_call | solution.py:305
  59.4 0.7 %copy.14 = f32[2,16,8,256]{3,2,1,0:T(8,128)} copy(f32[2,16,8,256]{3,2,1,0:T(8,128)S(1)} %picard.1) | data formatting | bytes 524288
Async XLA Ops:
  0.0 1.9 %copy-start.1 = (f32[16,8,256]{2,1,0:T(8,128)S(1)}, f32[16,8,256]{2,1,0:T(8,128)}, u32[]{:S(2)}) copy-start(f32[16,8,256]{2,1,0:T(8,128)} %start_ref.1) | copy-start | bytes 393220
  0.8 1.1 %copy-start.2 = (f32[3,3,16,128]{3,2,1,0:T(8,128)S(1)}, f32[3,3,16,128]{3,2,1,0:T(8,128)}, u32[]{:S(2)}) copy-start(f32[3,3,16,128]{3,2,1,0:T(8,128)} %wout_ref.1) | copy-start | bytes 221188
  0.8 1.1 %copy-start.3 = (f32[2,128]{1,0:T(2,128)S(1)}, f32[2,128]{1,0:T(2,128)}, u32[]{:S(2)}) copy-start(f32[2,128]{1,0:T(2,128)} %te_ref.1) | copy-start | bytes 3076
  0.8 1.1 %copy-start.4 = (f32[2]{0:T(128)S(1)}, f32[2]{0:T(128)}, u32[]{:S(2)}) copy-start(f32[2]{0:T(128)} %dx_ref.1) | copy-start | bytes 28
  0.8 1.1 %copy-start.5 = (f32[2]{0:T(128)S(1)}, f32[2]{0:T(128)}, u32[]{:S(2)}) copy-start(f32[2]{0:T(128)} %de_ref.1) | copy-start | bytes 28
  0.8 1.1 %copy-start.6 = (f32[128]{0:T(128)S(1)}, f32[128]{0:T(128)}, u32[]{:S(2)}) copy-start(f32[128]{0:T(128)} %param.15) | copy-start | bytes 1540
  0.8 1.1 %copy-start.7 = (f32[128]{0:T(128)S(1)}, f32[128]{0:T(128)}, u32[]{:S(2)}) copy-start(f32[128]{0:T(128)} %param.17) | copy-start | bytes 1540
  1.9 1.1 %copy-start = (f32[3,3,128,128]{3,2,1,0:T(8,128)S(1)}, f32[3,3,128,128]{3,2,1,0:T(8,128)}, u32[]{:S(2)}) copy-start(f32[3,3,128,128]{3,2,1,0:T(8,128)} %wmid_ref.1) | copy-start | bytes 1769476

commit v2 on v1

--- a/solution.py
+++ b/solution.py
@@ -7,6 +7,7 @@
 from jax.sharding import PartitionSpec as P
 
 HALO = 3
+UNROLL = 4
 BF = jnp.bfloat16
 F32 = jnp.float32
 
@@ -46,7 +47,7 @@
 
 
 def picard_kernel(start_ref, te_ref, dx_ref, de_ref, win_ref, bin_ref, wmid_ref, bmid_ref, wout_ref, bout_ref,
-                  out_ref, w0, w1, w2, bias, s0h, s0l, s1h, s1l, acc, x0, xin, run, car, snd, run2, car2, snd2,
+                  out_ref, w0, w1, w2, bias, s0h, s0l, s1h, s1l, h2, acc, x0, xin, run, car, snd, run2, car2, snd2,
                   hs_send, hs_recv, hr_send, hr_recv, c_send, c_recv, f_send, f_recv):
     states, chans, rows, cols = out_ref.shape
     hid = wmid_ref.shape[2]
@@ -156,54 +157,72 @@
 
     def network(fields):
         acc[...] = jnp.zeros_like(acc)
-
-        def first(r):
-            k0 = 3 * chans
-            at = pl.multiple_of(r * k0, 16)
-            grow = base + r - (HALO - 1)
-            keep = jnp.where((grow >= 0) & (grow < height), 1.0, 0.0).astype(F32)
-            for t in range(states):
-                if t < fields:
-                    f = dot(w0[...], s0h[t, pl.ds(at, 3 * k0), :])
-                    pre = f[:hid] + f[hid:] + dot(w0[0:hid, :], s0l[t, pl.ds(at, 3 * k0), :])
-                h = silu(pre + wide(bias[t], cols)) * keep
-                parts = shifted(h)
-                for b in range(3):
-                    hi, lo = split(parts[b])
-                    to = pl.multiple_of(r * 3 * hid + b * hid, 128)
-                    s1h[t, pl.ds(to, hid), :] = hi
-                    s1l[t, pl.ds(to, hid), :] = lo
-
-        def second(q):
-            k1 = 3 * hid
-            at = pl.multiple_of(q * k1, 128)
-            grow = base + q - (HALO - 2)
-            keep = jnp.where((grow >= 0) & (grow < height), 1.0, 0.0).astype(F32)
-            for t in range(states):
-                f = dot(w1[...], s1h[t, pl.ds(at, 3 * k1), :])
-                pre = f[:hid] + f[hid:] + dot(w1[0:hid, :], s1l[t, pl.ds(at, 3 * k1), :])
-                h = silu(pre + wide(bias[states], cols)) * keep
-                hi, lo = split(h)
-                g = dot(w2[...], jnp.concatenate([hi, lo], axis=0))
-                g = g[:taps] + g[taps:]
-                third = taps // 3
-                left, _, _ = shifted(g[:third])
-                _, _, right = shifted(g[2 * third:])
-                to = pl.multiple_of(q * chans, 16)
-                acc[t, pl.ds(to, third), :] += left + g[third:2 * third] + right
-
-        def lap0(r, c):
-            first(r)
+        k0, k1, third = 3 * chans, 3 * hid, taps // 3
+
+        def inside(row):
+            return jnp.where((base + row >= 0) & (base + row < height), 1.0, 0.0).astype(F32)
+
+        def first_dot(t, r):
+            at = pl.ds(pl.multiple_of(r * k0, 16), 3 * k0)
+            f = dot(w0[...], s0h[t, at, :])
+            return f[:hid] + f[hid:] + dot(w0[0:hid, :], s0l[t, at, :])
+
+        def first_end(t, r, pre):
+            h = silu(pre + wide(bias[t], cols)) * inside(r - (HALO - 1))
+            parts = shifted(h)
+            for b in range(3):
+                hi, lo = split(parts[b])
+                to = pl.ds(pl.multiple_of(r * k1 + b * hid, 128), hid)
+                s1h[t][to, :] = hi
+                s1l[t][to, :] = lo
+
+        def mid_dot(t, q):
+            at = pl.ds(pl.multiple_of(q * k1, 128), 3 * k1)
+            f = dot(w1[...], s1h[t][at, :])
+            return f[:hid] + f[hid:] + dot(w1[0:hid, :], s1l[t][at, :])
+
+        def mid_end(t, q, pre):
+            h = silu(pre + wide(bias[states], cols)) * inside(q - (HALO - 2))
+            hi, lo = split(h)
+            h2[t][0:hid, :] = hi
+            h2[t][hid:2 * hid, :] = lo
+
+        def last_conv(t, q):
+            g = dot(w2[...], h2[t][...])
+            g = g[:taps] + g[taps:]
+            left, _, _ = shifted(g[:third])
+            _, _, right = shifted(g[2 * third:])
+            to = pl.ds(pl.multiple_of(q * chans, 16), third)
+            acc[t, to, :] += left + g[third:2 * third] + right
+
+        def stage(r, with_first=True, with_mid=True, with_last=True):
+            firsts, mids = {}, {}
+            for t in range(states):
+                if with_first:
+                    firsts[t] = first_dot(t, r) if t < fields else firsts[0]
+            for t in range(states):
+                if with_mid:
+                    mids[t] = mid_dot(t, r - 3)
+                if with_last:
+                    last_conv(t, r - 4)
+                if with_first:
+                    first_end(t, r, firsts[t])
+                if with_mid:
+                    mid_end(t, r - 3, mids[t])
+
+        def fill(r, c):
+            stage(r, True, False, False)
             return c
 
         def lap(r, c):
-            second(r - 3)
-            first(r)
+            stage(r)
             return c
 
-        lax.fori_loop(0, 3, lap0, 0)
-        lax.fori_loop(3, rows + 4, lap, 0)
-        second(rows + 1)
+        lax.fori_loop(0, 3, fill, 0)
+        stage(3, True, True, False)
+        lax.fori_loop(4, rows + 4, lap, 0, unroll=UNROLL)
+        stage(rows + 4, False, True, True)
+        stage(rows + 5, False, False, True)
 
     def drifts(put, source):
         bo = wide(bout_ref[...], cols)
@@ -314,8 +333,9 @@
             pltpu.VMEM((states + 1, hid, 128), F32),
             pltpu.VMEM((states, ext * 3 * chans, cols), BF),
             pltpu.VMEM((states, ext * 3 * chans, cols), BF),
-            pltpu.VMEM((states, (rows + 4) * 3 * hid, cols), BF),
-            pltpu.VMEM((states, (rows + 4) * 3 * hid, cols), BF),
+            [pltpu.VMEM(((rows + 4) * 3 * hid, cols), BF)] * states,
+            [pltpu.VMEM(((rows + 4) * 3 * hid, cols), BF)] * states,
+            [pltpu.VMEM((2 * hid, cols), BF)] * states,
             pltpu.VMEM((states, (rows + 4) * chans, cols), F32),
             pltpu.VMEM((ext, chans, cols), F32),
             pltpu.VMEM((states, ext, chans, cols), F32),

time: 60.3 us -> 40.9 us (0.68)
  Pallas kernels: 56.4 us -> 36.9 us
    pallas_call x1, Pallas kernels: 56.4 us -> 36.9 us  [picard(): pl.pallas_call(picard_kernel, out_shape=jax.ShapeDtypeStruct((states, cha...]
where the time goes in v2:
time: 40.9 us; the launch traced here: 40.7 us
  Pallas kernels  36.9 us (90%)
  local copies, waits for them, and re-layouts  3.61 us (9%)
    pallas_call x1, Pallas kernels, picard(): pl.pallas_call(picard_kernel, out_shape=jax.ShapeDtypeStruct((states, cha...  36.9 us
    unnamed x17, local copies, waits for them, and re-layouts  1.8 us
    reshape x1, local copies, waits for them, and re-layouts, on_device(): win = jnp.transpose(w_in, (2, 0, 1, 3)).reshape(hid, 9 * chans)  1.05 us

profile of v2, /device:TPU:3, one launch (start us, length us, event | category | flops | bytes accessed | tf_op | source)
XLA Modules:
  0.0 40.7 jit_solution(1362327413236731519)
XLA Ops:
  0.0 0.0 copy-start.1
  0.0 0.8 %broadcast_in_dim.14.bout_ref = f32[16,128]{1,0:T(8,128)S(1)} broadcast(f32[16]{0:T(128)} %param.19), dimensions={0} | broadcast | bytes 8256 | tf_op jit(solution)/shard_map/broadcast_in_dim | solution.py:360
  0.8 0.0 copy-start.2
  0.8 0.0 copy-start.3
  0.8 0.0 copy-start.4
  0.8 0.0 copy-start.5
  0.8 0.0 copy-start.6
  0.8 0.0 copy-start.7
  0.8 1.1 %copy.12.win_ref = f32[128,144]{1,0:T(8,128)S(1)} copy(f32[128,144]{0,1:T(8,128)} %bitcast.7) | data formatting | bytes 147456 | tf_op jit(solution)/shard_map/reshape | solution.py:359
  1.9 0.0 copy-done.1
  1.9 0.0 copy-done.2
  1.9 0.0 copy-done.3
  1.9 0.0 copy-done.4
  1.9 0.0 copy-done.5
  1.9 0.0 copy-done.6
  1.9 0.0 copy-done.7
  1.9 0.0 copy-start
  1.9 1.1 %copy-done = f32[3,3,128,128]{3,2,1,0:T(8,128)S(1)} copy-done((f32[3,3,128,128]{3,2,1,0:T(8,128)S(1)}, f32[3,3,128,128]{3,2,1,0:T(8,128)}, u32[]{:S(2)}) %copy-start) | copy-done | bytes 589848
  3.0 36.9 %picard.1 = f32[2,16,8,256]{3,2,1,0:T(8,128)S(1)} custom-call(f32[16,8,256]{2,1,0:T(8,128)S(1)} %copy-done.1, f32[2,128]{1,0:T(2,128)S(1)} %copy-done.3, f32[2]{0:T(128)S(1)} %copy-done.4, f32[2]{0:T(128)S(1)} %copy-done.5, f32[128,144]{1,0:T(8,128)S(1)} %copy.12.win_ref, f32[1,128]{1,0:T(1,128)S(1)} %bitcast.5, f32[3,3,128,128]{3,2,1,0:T(8,128)S(1)} %copy-done, ...), custom_call_target="tpu_custom_call" | custom-call | tf_op jit(solution)/shard_map/picard/pallas_call | solution.py:324
  40.0 0.7 %copy.14 = f32[2,16,8,256]{3,2,1,0:T(8,128)} copy(f32[2,16,8,256]{3,2,1,0:T(8,128)S(1)} %picard.1) | data formatting | bytes 524288
Async XLA Ops:
  0.0 1.9 %copy-start.1 = (f32[16,8,256]{2,1,0:T(8,128)S(1)}, f32[16,8,256]{2,1,0:T(8,128)}, u32[]{:S(2)}) copy-start(f32[16,8,256]{2,1,0:T(8,128)} %start_ref.1) | copy-start | bytes 393220
  0.8 1.1 %copy-start.2 = (f32[3,3,16,128]{3,2,1,0:T(8,128)S(1)}, f32[3,3,16,128]{3,2,1,0:T(8,128)}, u32[]{:S(2)}) copy-start(f32[3,3,16,128]{3,2,1,0:T(8,128)} %wout_ref.1) | copy-start | bytes 221188
  0.8 1.1 %copy-start.3 = (f32[2,128]{1,0:T(2,128)S(1)}, f32[2,128]{1,0:T(2,128)}, u32[]{:S(2)}) copy-start(f32[2,128]{1,0:T(2,128)} %te_ref.1) | copy-start | bytes 3076
  0.8 1.1 %copy-start.4 = (f32[2]{0:T(128)S(1)}, f32[2]{0:T(128)}, u32[]{:S(2)}) copy-start(f32[2]{0:T(128)} %dx_ref.1) | copy-start | bytes 28
  0.8 1.1 %copy-start.5 = (f32[2]{0:T(128)S(1)}, f32[2]{0:T(128)}, u32[]{:S(2)}) copy-start(f32[2]{0:T(128)} %de_ref.1) | copy-start | bytes 28
  0.8 1.1 %copy-start.6 = (f32[128]{0:T(128)S(1)}, f32[128]{0:T(128)}, u32[]{:S(2)}) copy-start(f32[128]{0:T(128)} %param.15) | copy-start | bytes 1540
  0.8 1.1 %copy-start.7 = (f32[128]{0:T(128)S(1)}, f32[128]{0:T(128)}, u32[]{:S(2)}) copy-start(f32[128]{0:T(128)} %param.17) | copy-start | bytes 1540
  1.9 1.1 %copy-start = (f32[3,3,128,128]{3,2,1,0:T(8,128)S(1)}, f32[3,3,128,128]{3,2,1,0:T(8,128)}, u32[]{:S(2)}) copy-start(f32[3,3,128,128]{3,2,1,0:T(8,128)} %wmid_ref.1) | copy-start | bytes 1769476

commit v3 on v2

--- a/solution.py
+++ b/solution.py
@@ -47,7 +47,7 @@
 
 
 def picard_kernel(start_ref, te_ref, dx_ref, de_ref, win_ref, bin_ref, wmid_ref, bmid_ref, wout_ref, bout_ref,
-                  out_ref, w0, w1, w2, bias, s0h, s0l, s1h, s1l, h2, acc, x0, xin, run, car, snd, run2, car2, snd2,
+                  out_ref, bo_ref, w0, w1, w2, bias, s0h, s0l, s1h, s1l, h2, acc, x0, xin, run, car, snd, run2, car2, snd2,
                   hs_send, hs_recv, hr_send, hr_recv, c_send, c_recv, f_send, f_recv):
     states, chans, rows, cols = out_ref.shape
     hid = wmid_ref.shape[2]
@@ -122,9 +122,11 @@
     run_halo = ((run, hr_send, hr_recv), (slice(None),))
     halo_start(*start_halo)
 
-    hi, lo = split(win_ref[...])
+    hi, lo = split(jnp.transpose(win_ref[...]))
     w0[0:hid, :] = hi
     w0[hid:2 * hid, :] = lo
+    bias_out = column(bout_ref[...], 128)
+    bo_ref[...] = bias_out
     for a in range(3):
         for b in range(3):
             hi, lo = split(wmid_ref[a, b])
@@ -218,14 +220,14 @@
             stage(r)
             return c
 
-        lax.fori_loop(0, 3, fill, 0)
+        lax.fori_loop(0, 3, fill, 0, unroll=3)
         stage(3, True, True, False)
         lax.fori_loop(4, rows + 4, lap, 0, unroll=UNROLL)
         stage(rows + 4, False, True, True)
         stage(rows + 5, False, False, True)
 
     def drifts(put, source):
-        bo = wide(bout_ref[...], cols)
+        bo = wide(bo_ref[...], cols)
         for h in range(rows):
             total = None
             for t in range(states):
@@ -327,6 +329,7 @@
         in_specs=[vm, vm, sm, sm, vm, vm, vm, vm, vm, vm],
         out_specs=vm,
         scratch_shapes=[
+            pltpu.VMEM((chans, 128), F32),
             pltpu.VMEM((2 * hid, 9 * chans), BF),
             pltpu.VMEM((2 * hid, 9 * hid), BF),
             pltpu.VMEM((18 * chans, 2 * hid), BF),
@@ -354,11 +357,9 @@
 
 
 def on_device(start_latent, time_embed, drift_x, drift_eps, w_in, b_in, w_mid, b_mid, w_out, b_out):
-    chans = start_latent.shape[0]
-    hid = w_mid.shape[2]
-    win = jnp.transpose(w_in, (2, 0, 1, 3)).reshape(hid, 9 * chans)
-    bout = jnp.broadcast_to(b_out[:, None], (chans, 128))
-    return picard(start_latent, time_embed, drift_x, drift_eps, win, b_in[None], w_mid, b_mid[None], w_out, bout)
+    hid, chans = w_in.shape[2:]
+    w_in = jnp.transpose(w_in, (0, 1, 3, 2)).reshape(9 * chans, hid)
+    return picard(start_latent, time_embed, drift_x, drift_eps, w_in, b_in[None], w_mid, b_mid[None], w_out, b_out[None])
 
 
 def solution(mesh):

time: 40.9 us -> 41.1 us (level)
  local copies, waits for them, and re-layouts: 3.61 us -> 5.15 us
  Pallas kernels: 36.9 us -> 35.7 us
    unnamed x17 -> x21, local copies, waits for them, and re-layouts: 1.8 us -> 5.15 us
    pallas_call x1, Pallas kernels: 36.9 us -> 35.7 us  [picard(): pl.pallas_call(picard_kernel, out_shape=jax.ShapeDtypeStruct((states, cha...]
    reshape x1 -> x0, local copies, waits for them, and re-layouts: 1.05 us -> none  [on_device(): win = jnp.transpose(w_in, (2, 0, 1, 3)).reshape(hid, 9 * chans)]
    broadcast_in_dim x1 -> x0, local copies, waits for them, and re-layouts: 0.76 us -> none  [on_device(): bout = jnp.broadcast_to(b_out[:, None], (chans, 128))]
where the time goes in v3:
time: 41.1 us; the launch traced here: 40.9 us
  Pallas kernels  35.7 us (87%)
  local copies, waits for them, and re-layouts  5.15 us (13%)
    pallas_call x1, Pallas kernels, picard(): pl.pallas_call(picard_kernel, out_shape=jax.ShapeDtypeStruct((states, cha...  35.7 us
    unnamed x21, local copies, waits for them, and re-layouts  5.15 us

profile of v3, /device:TPU:3, one launch (start us, length us, event | category | flops | bytes accessed | tf_op | source)
XLA Modules:
  0.0 40.9 jit_solution(6157409614997624850)
XLA Ops:
  0.0 0.0 copy-start.6
  0.0 0.0 copy-start.7
  0.0 0.0 copy-start.8
  0.0 0.0 copy-start.9
  0.0 0.0 copy-start.4
  0.0 0.0 copy-start.5
  0.0 0.6 %copy-done.6 = f32[2]{0:T(128)S(1)} copy-done((f32[2]{0:T(128)S(1)}, f32[2]{0:T(128)}, u32[]{:S(2)}) %copy-start.6) | copy-done | bytes 32
  0.7 0.0 copy-done.7
  0.7 0.0 copy-done.8
  0.7 0.0 copy-done.9
  0.7 0.0 copy-done.4
  0.7 0.0 copy-done.5
  0.7 0.0 copy-start
  0.7 1.1 %copy-done = f32[3,3,128,128]{3,2,1,0:T(8,128)S(1)} copy-done((f32[3,3,128,128]{3,2,1,0:T(8,128)S(1)}, f32[3,3,128,128]{3,2,1,0:T(8,128)}, u32[]{:S(2)}) %copy-start) | copy-done | bytes 589848
  1.8 0.0 copy-start.1
  1.8 0.9 %copy-done.1 = f32[16,8,256]{2,1,0:T(8,128)S(1)} copy-done((f32[16,8,256]{2,1,0:T(8,128)S(1)}, f32[16,8,256]{2,1,0:T(8,128)}, u32[]{:S(2)}) %copy-start.1) | copy-done | bytes 131096
  2.7 0.0 copy-start.2
  2.7 0.9 %copy-done.2 = f32[3,3,128,16]{2,3,1,0:T(8,128)S(1)} copy-done((f32[3,3,128,16]{2,3,1,0:T(8,128)S(1)}, f32[3,3,128,16]{2,3,1,0:T(8,128)}, u32[]{:S(2)}) %copy-start.2) | copy-done | bytes 73752
  3.6 0.0 copy-start.3
  3.6 0.9 %copy-done.3 = f32[3,3,16,128]{3,2,1,0:T(8,128)S(1)} copy-done((f32[3,3,16,128]{3,2,1,0:T(8,128)S(1)}, f32[3,3,16,128]{3,2,1,0:T(8,128)}, u32[]{:S(2)}) %copy-start.3) | copy-done | bytes 73752
  4.5 35.7 %picard.1 = f32[2,16,8,256]{3,2,1,0:T(8,128)S(1)} custom-call(f32[16,8,256]{2,1,0:T(8,128)S(1)} %copy-done.1, f32[2,128]{1,0:T(2,128)S(1)} %copy-done.4, f32[2]{0:T(128)S(1)} %copy-done.5, f32[2]{0:T(128)S(1)} %copy-done.6, f32[144,128]{1,0:T(8,128)S(1)} %bitcast.6, f32[1,128]{1,0:T(1,128)S(1)} %bitcast.7, f32[3,3,128,128]{3,2,1,0:T(8,128)S(1)} %copy-done, ...), custom_call_target="tpu_custom_call" | custom-call | tf_op jit(solution)/shard_map/picard/pallas_call | solution.py:326
  40.1 0.7 %copy.12 = f32[2,16,8,256]{3,2,1,0:T(8,128)} copy(f32[2,16,8,256]{3,2,1,0:T(8,128)S(1)} %picard.1) | data formatting | bytes 524288
Async XLA Ops:
  0.0 0.7 %copy-start.6 = (f32[2]{0:T(128)S(1)}, f32[2]{0:T(128)}, u32[]{:S(2)}) copy-start(f32[2]{0:T(128)} %de_ref.1) | copy-start | bytes 28
  0.0 0.7 %copy-start.7 = (f32[128]{0:T(128)S(1)}, f32[128]{0:T(128)}, u32[]{:S(2)}) copy-start(f32[128]{0:T(128)} %param.15) | copy-start | bytes 1540
  0.0 0.7 %copy-start.8 = (f32[128]{0:T(128)S(1)}, f32[128]{0:T(128)}, u32[]{:S(2)}) copy-start(f32[128]{0:T(128)} %param.17) | copy-start | bytes 1540
  0.0 0.7 %copy-start.9 = (f32[16]{0:T(128)S(1)}, f32[16]{0:T(128)}, u32[]{:S(2)}) copy-start(f32[16]{0:T(128)} %param.19) | copy-start | bytes 196
  0.0 0.7 %copy-start.4 = (f32[2,128]{1,0:T(2,128)S(1)}, f32[2,128]{1,0:T(2,128)}, u32[]{:S(2)}) copy-start(f32[2,128]{1,0:T(2,128)} %te_ref.1) | copy-start | bytes 3076
  0.0 0.7 %copy-start.5 = (f32[2]{0:T(128)S(1)}, f32[2]{0:T(128)}, u32[]{:S(2)}) copy-start(f32[2]{0:T(128)} %dx_ref.1) | copy-start | bytes 28
  0.7 1.1 %copy-start = (f32[3,3,128,128]{3,2,1,0:T(8,128)S(1)}, f32[3,3,128,128]{3,2,1,0:T(8,128)}, u32[]{:S(2)}) copy-start(f32[3,3,128,128]{3,2,1,0:T(8,128)} %wmid_ref.1) | copy-start | bytes 1769476
  1.8 0.9 %copy-start.1 = (f32[16,8,256]{2,1,0:T(8,128)S(1)}, f32[16,8,256]{2,1,0:T(8,128)}, u32[]{:S(2)}) copy-start(f32[16,8,256]{2,1,0:T(8,128)} %start_ref.1) | copy-start | bytes 393220
  2.7 0.9 %copy-start.2 = (f32[3,3,128,16]{2,3,1,0:T(8,128)S(1)}, f32[3,3,128,16]{2,3,1,0:T(8,128)}, u32[]{:S(2)}) copy-start(f32[3,3,128,16]{2,3,1,0:T(8,128)} %param.14) | copy-start | bytes 221188
  3.6 0.9 %copy-start.3 = (f32[3,3,16,128]{3,2,1,0:T(8,128)S(1)}, f32[3,3,16,128]{3,2,1,0:T(8,128)}, u32[]{:S(2)}) copy-start(f32[3,3,16,128]{3,2,1,0:T(8,128)} %wout_ref.1) | copy-start | bytes 221188
